TPU v7x, 512 devices: a whole 4x4x16 slice. The times are simulated.
512 devices in a mesh: seq: 64 (over z, y), tp: 8 (over x, core).
Axes of the slice: x: 4, y: 4, z: 16, core: 2. Of those that a mesh axis runs over, the one named last changes fastest.
Arguments:
- hidden: bfloat16 [384, 2048], P(None, 'seq'), may hold values from -12 to 12
- ln1_gain: float32 [2048], P('seq'), may hold values from 0.1 to 1.9
- wq: bfloat16 [2048, 2048], P('seq', 'tp'), may hold values from -0.125 to 0.125
- wk: bfloat16 [2048, 1024], P('seq', 'tp'), may hold values from -0.125 to 0.125
- wv: bfloat16 [2048, 1024], P('seq', 'tp'), may hold values from -0.125 to 0.125
- wg: bfloat16 [2048, 2048], P('seq', 'tp'), may hold values from -0.125 to 0.125
- q_gain: float32 [128], replicated, may hold values from 1 to 30
- key_gain: float32 [128], replicated, may hold values from 0.5 to 1.5
- wo: bfloat16 [2048, 2048], P('tp', 'seq'), may hold values from -0.5 to 0.5
- ln2_gain: float32 [2048], P('seq'), may hold values from 0.1 to 1.9
- w_gate: bfloat16 [2048, 6144], P('seq', 'tp'), may hold values from -0.125 to 0.125
- w_up: bfloat16 [2048, 6144], P('seq', 'tp'), may hold values from -0.125 to 0.125
- w_down: bfloat16 [6144, 2048], P('tp', 'seq'), may hold values from -0.078125 to 0.078125
- last_gain: float32 [2048], P('seq'), may hold values from 0.1 to 1.9
- head_weight: bfloat16 [2048, 131072], P(None, ('seq', 'tp')), may hold values from -0.125 to 0.125
- inv_temp: float32 [8], replicated, may hold values from 0.5 to 64
- key_cache: bfloat16 [8, 16384, 1024], P(None, 'seq', 'tp'), may hold values from -40 to 40
- value_cache: bfloat16 [8, 16384, 1024], P(None, 'seq', 'tp'), may hold values from -6 to 6
- lengths: int32 [8], replicated, may hold values from 1 to 16336
- parents: int32 [8, 48], replicated, may hold values from 0 to 46, as said below
- accepted: int32 [8], replicated, may hold values from 0 to 47
Outputs:
- logprobs: float32 [384, 131072], P(None, ('seq', 'tp'))
- next_hidden: bfloat16 [384, 2048], P(None, 'seq')
- updated_key_cache: bfloat16 [8, 16384, 1024], P(None, 'seq', 'tp')
- updated_value_cache: bfloat16 [8, 16384, 1024], P(None, 'seq', 'tp')
Inputs may be any that keep to these rules, and one draw needn't show every extreme that they name: parents[r, 0] = 0; for i >= 1, i - 4 <= parents[r, i] < i.
All inputs are finite; a program needn't handle non-finite values.
Results may differ from a plain program's by a relative error of at most 0.012.
Values may be sent and summed in bfloat16 or wider, within the bound.
No kernel may reach another device: no remote copies, remote signals or barrier semaphores. Data moves between devices by JAX's collectives and lax.ppermute only.
A program may use at most 128 MiB of HBM per device.

v0:
```python
import jax
import jax.numpy as jnp
from jax import lax
from jax.sharding import PartitionSpec as P

EPSILON = 1e-06
ROPE_BASE = 1000000.0
NEGATIVE = -1e30


def ancestry(parents):
    node_count = parents.shape[-1]
    node_ids = jnp.arange(node_count, dtype=jnp.int32)
    reachable = (parents[..., :, None] == node_ids[None, :]).astype(jnp.float32)
    reachable = jnp.maximum(reachable, jnp.eye(node_count, dtype=jnp.float32))
    for turn in range((node_count - 1).bit_length()):
        reachable = jnp.minimum(
            jnp.einsum("rij,rjk->rik", reachable, reachable, precision=lax.Precision.HIGHEST), 1.0
        )
    return reachable


def head_norm(values, gain):
    meansq = jnp.mean(values * values, axis=-1, keepdims=True)
    return values * lax.rsqrt(meansq + EPSILON) * gain


def apply_rotary(values, places):
    half_dim = values.shape[-1] // 2
    spread = ROPE_BASE ** (-jnp.arange(half_dim, dtype=jnp.float32) / half_dim)
    angles = places.astype(jnp.float32)[:, None] * spread[None, :]
    cosine = jnp.cos(angles)[:, None, :]
    sine = jnp.sin(angles)[:, None, :]
    lower_part = values[..., :half_dim]
    upper_part = values[..., half_dim:]
    return jnp.concatenate(
        [lower_part * cosine - upper_part * sine, upper_part * cosine + lower_part * sine], axis=-1
    )


def cache_part(query_blocks, key_block, value_block, valid_slot):
    scores = jnp.einsum(
        "rikgd,rckd->rkgic", query_blocks, key_block, preferred_element_type=jnp.float32
    )
    valid_slot = valid_slot[:, None, None, None, :]
    row_peak = jnp.max(jnp.where(valid_slot, scores, NEGATIVE), axis=-1)
    weights = jnp.where(valid_slot, jnp.exp(scores - row_peak[..., None]), 0.0)
    row_mass = jnp.sum(weights, axis=-1)
    weighted = jnp.einsum(
        "rkgic,rckd->rkgid",
        weights.astype(jnp.bfloat16),
        value_block,
        preferred_element_type=jnp.float32,
    )
    return (row_peak, row_mass, weighted)


def on_device(
    hidden,
    ln1_gain,
    wq,
    wk,
    wv,
    wg,
    q_gain,
    key_gain,
    wo,
    ln2_gain,
    w_gate,
    w_up,
    w_down,
    last_gain,
    head_weight,
    inv_temp,
    key_cache,
    value_cache,
    lengths,
    parents,
    accepted,
):
    seq_count = lax.axis_size("seq")
    model_width = hidden.shape[1] * seq_count
    head_dim = q_gain.shape[0]
    query_heads = wq.shape[1] // head_dim
    kv_heads = wk.shape[1] // head_dim
    query_group_size = query_heads // kv_heads
    requests, tree_size = parents.shape
    token_count = hidden.shape[0]
    slot_count = key_cache.shape[1]
    slot_start = lax.axis_index("seq") * slot_count
    parent_links = ancestry(parents)
    tree_node_depth = jnp.sum((parent_links > 0.5).astype(jnp.int32), axis=-1) - 1
    token_position = (lengths[:, None] + tree_node_depth).reshape(-1)
    hidden_wide = hidden.astype(jnp.float32)
    squares = lax.psum(jnp.sum(hidden_wide * hidden_wide, axis=1), "seq")
    normed1 = (hidden_wide * lax.rsqrt(squares / model_width + EPSILON)[:, None] * ln1_gain).astype(
        jnp.bfloat16
    )
    q_sum, key_sum, v_sum, gate = lax.psum(
        (
            jnp.dot(normed1, wq, preferred_element_type=jnp.float32),
            jnp.dot(normed1, wk, preferred_element_type=jnp.float32),
            jnp.dot(normed1, wv, preferred_element_type=jnp.float32),
            jnp.dot(normed1, wg, preferred_element_type=jnp.float32),
        ),
        "seq",
    )
    query_rows_all = apply_rotary(
        head_norm(q_sum.reshape(token_count, query_heads, head_dim), q_gain), token_position
    ) * head_dim ** (-0.5)
    query_rows_all = query_rows_all.astype(jnp.bfloat16).reshape(
        requests, tree_size, kv_heads, query_group_size, head_dim
    )
    draft_keys = apply_rotary(
        head_norm(key_sum.reshape(token_count, kv_heads, head_dim), key_gain), token_position
    ).astype(jnp.bfloat16)
    draft_values = v_sum.astype(jnp.bfloat16)
    tree_keys = draft_keys.reshape(requests, tree_size, kv_heads, head_dim)
    tree_values = draft_values.reshape(requests, tree_size, kv_heads, head_dim)
    cache_keys = key_cache.reshape(requests, slot_count, kv_heads, head_dim)
    cache_values = value_cache.reshape(requests, slot_count, kv_heads, head_dim)
    slot_ids = slot_start + jnp.arange(slot_count, dtype=jnp.int32)
    local_state = cache_part(
        query_rows_all, cache_keys, cache_values, slot_ids[None, :] < lengths[:, None]
    )
    local_peak, local_mass, local_sum = local_state
    cache_peak = lax.pmax(local_peak, "seq")
    factor = jnp.exp(local_peak - cache_peak)
    cache_mass, cache_sum = lax.psum((local_mass * factor, local_sum * factor[..., None]), "seq")
    tree_scores = jnp.einsum(
        "rikgd,rjkd->rkgij", query_rows_all, tree_keys, preferred_element_type=jnp.float32
    )
    valid_node = (parent_links > 0.5)[:, None, None, :, :]
    row_top = jnp.maximum(
        cache_peak, jnp.max(jnp.where(valid_node, tree_scores, NEGATIVE), axis=-1)
    )
    tree_weights = jnp.where(valid_node, jnp.exp(tree_scores - row_top[..., None]), 0.0)
    cache_factor = jnp.exp(cache_peak - row_top)
    row_mass = cache_mass * cache_factor + jnp.sum(tree_weights, axis=-1)
    weighted = cache_sum * cache_factor[..., None] + jnp.einsum(
        "rkgij,rjkd->rkgid",
        tree_weights.astype(jnp.bfloat16),
        tree_values,
        preferred_element_type=jnp.float32,
    )
    attention_result = jnp.transpose(weighted / row_mass[..., None], (0, 3, 1, 2, 4)).reshape(
        token_count, query_heads * head_dim
    )
    gated = (attention_result * jax.nn.sigmoid(gate)).astype(jnp.bfloat16)
    attn_sum = lax.psum(jnp.dot(gated, wo, preferred_element_type=jnp.float32), "tp")
    middle = (hidden_wide + attn_sum).astype(jnp.bfloat16)
    middle_wide = middle.astype(jnp.float32)
    squares_mid = lax.psum(jnp.sum(middle_wide * middle_wide, axis=1), "seq")
    normed2 = (
        middle_wide * lax.rsqrt(squares_mid / model_width + EPSILON)[:, None] * ln2_gain
    ).astype(jnp.bfloat16)
    gate_part, up_part = lax.psum(
        (
            jnp.dot(normed2, w_gate, preferred_element_type=jnp.float32),
            jnp.dot(normed2, w_up, preferred_element_type=jnp.float32),
        ),
        "seq",
    )
    activated = (jax.nn.silu(gate_part) * up_part).astype(jnp.bfloat16)
    down_part = jnp.dot(activated, w_down, preferred_element_type=jnp.float32)
    down_sum = lax.psum(down_part, "tp")
    next_hidden = (middle_wide + down_sum).astype(jnp.bfloat16)
    next_wide = next_hidden.astype(jnp.float32)
    squares_last = lax.psum(jnp.sum(next_wide * next_wide, axis=1), "seq")
    normed3 = (
        next_wide * lax.rsqrt(squares_last / model_width + EPSILON)[:, None] * last_gain
    ).astype(jnp.bfloat16)
    logits = jnp.dot(
        lax.all_gather(normed3, "seq", axis=1, tiled=True),
        head_weight,
        preferred_element_type=jnp.float32,
    )
    logits = logits * jnp.repeat(inv_temp, tree_size)[:, None]
    vocab_top = lax.pmax(jnp.max(logits, axis=1), ("seq", "tp"))
    vocab_total = lax.psum(jnp.sum(jnp.exp(logits - vocab_top[:, None]), axis=1), ("seq", "tp"))
    logprobs = logits - (vocab_top + jnp.log(vocab_total))[:, None]
    accepted_rows = parent_links[jnp.arange(requests), accepted]
    target = token_position.reshape(requests, tree_size)
    slot_all = slot_start + jnp.arange(slot_count, dtype=jnp.int32)
    placed = (slot_all[None, :, None] == target[:, None, :]).astype(jnp.float32) * accepted_rows[
        :, None, :
    ]
    hits = (jnp.sum(placed, axis=2) > 0.5)[:, :, None]
    placed_low = placed.astype(jnp.bfloat16)
    moved_keys = jnp.einsum(
        "rca,rae->rce",
        placed_low,
        draft_keys.reshape(requests, tree_size, kv_heads * head_dim),
        preferred_element_type=jnp.float32,
    ).astype(jnp.bfloat16)
    moved_values = jnp.einsum(
        "rca,rae->rce",
        placed_low,
        draft_values.reshape(requests, tree_size, kv_heads * head_dim),
        preferred_element_type=jnp.float32,
    ).astype(jnp.bfloat16)
    updated_key_cache = jnp.where(hits, moved_keys, key_cache)
    updated_value_cache = jnp.where(hits, moved_values, value_cache)
    return (logprobs, next_hidden, updated_key_cache, updated_value_cache)


def solution(mesh):
    in_specs = (
        P(None, "seq"),
        P("seq"),
        P("seq", "tp"),
        P("seq", "tp"),
        P("seq", "tp"),
        P("seq", "tp"),
        P(),
        P(),
        P("tp", "seq"),
        P("seq"),
        P("seq", "tp"),
        P("seq", "tp"),
        P("tp", "seq"),
        P("seq"),
        P(None, ("seq", "tp")),
        P(),
        P(None, "seq", "tp"),
        P(None, "seq", "tp"),
        P(),
        P(),
        P(),
    )
    out_specs = (P(None, ("seq", "tp")), P(None, "seq"), P(None, "seq", "tp"), P(None, "seq", "tp"))
    return jax.shard_map(
        on_device, mesh=mesh, in_specs=in_specs, out_specs=out_specs, check_vma=False
    )
```

profile of v0, /device:TPU:1, one launch (start us, length us, event | category | flops | bytes accessed | tf_op | source)
XLA Modules:
  0.0 1792.0 jit_solution(4256023891018787633)
XLA Ops:
  8.1 122.9 %psum.98 = f32[384]{0:T(512)S(1)} all-reduce(f32[384]{0:T(512)S(1)} %fusion.51), channel_id=1, replica_groups=mesh['seq'=64,'tp'=8] {'seq'}, use_global_device_ids=true, to_apply=%region_1.0 | all-reduce | flops 384 | bytes 3072 | tf_op jit(solution)/shard_map/psum | solution.py:95
  130.9 1.8 fusion.88
  132.8 1.4 convolution_minimum_fusion.5
  138.7 269.0 %all-reduce.8.cloned.1.call-done = f32[384,2,128]{0,2,1:T(8,128)} async-done(((f32[384,2,128]{0,2,1:T(8,128)}), f32[384,2,128]{0,2,1:T(8,128)}) %all-reduce.8.cloned.1.call-update) | async-done | bytes 393232 | tf_op jit(solution)/shard_map/psum | solution.py:99
  408.8 1.1 multiply_multiply_fusion
  411.8 114.2 %pmax.14 = f32[8,1,2,48]{3,2,0,1:T(2,128)S(1)} all-reduce(f32[8,1,2,48]{3,2,0,1:T(2,128)S(1)} %bitcast.134), channel_id=1, replica_groups=mesh['seq'=64,'tp'=8] {'seq'}, use_global_device_ids=true, to_apply=%region_6.0 | all-reduce | flops 768 | bytes 6144 | tf_op jit(solution)/shard_map/pmax | solution.py:127
  526.5 1.1 fusion.2
  528.0 219.4 %all-reduce.13 = (bf16[384,128]{1,0:T(8,128)(2,1)S(1)}, f32[8,1,2,48]{3,2,0,1:T(2,128)S(1)}) all-reduce(f32[384,128]{1,0:T(8,128)S(1)} %fusion.84, f32[8,1,2,48]{3,2,0,1:T(2,128)S(1)} %get-tuple-element.32), channel_id=1, replica_groups=mesh['seq'=64,'tp'=8] {'seq'}, use_global_device_ids=true, to_apply=%region_11.12 | all-reduce | flops 49920 | bytes 301056 | tf_op jit(solution)/shard_map/psum | solution.py:99
  747.3 74.5 %all-reduce.12.cloned.1.call-done = (f32[8,1,2,48,128]{4,3,2,0,1:T(8,128)}, f32[384,128]{1,0:T(8,128)}, f32[384,256]{1,0:T(8,128)}) async-done(((f32[8,1,2,48,128]{4,3,2,0,1:T(8,128)}, f32[384,128]{1,0:T(8,128)}, f32[384,256]{1,0:T(8,128)}), (f32[8,1,2,48,128]{4,3,2,0,1:T(8,128)}, f32[384,128]{1,0:T(8,128)}, f32[384,256]{1,0:T(8,128)})) %all-reduce.12.cloned.1.call-update) | async-done | bytes 983056 | tf_op jit(solution)/shard_map/psum | solution.py:129
  822.9 1.1 multiply_bitcast_fusion
  826.7 39.8 %psum.105 = f32[384,32]{0,1:T(8,128)S(1)} all-reduce(f32[384,32]{0,1:T(8,128)S(1)} %fusion.43), channel_id=1, replica_groups=mesh['seq'=64,'tp'=8] {'tp'}, use_global_device_ids=true, to_apply=%region_16.17 | all-reduce | flops 12288 | bytes 98304 | tf_op jit(solution)/shard_map/psum | solution.py:150
  866.5 110.1 %psum.106 = f32[384]{0:T(512)S(1)} all-reduce(f32[384]{0:T(512)S(1)} %get-tuple-element.21), channel_id=1, replica_groups=mesh['seq'=64,'tp'=8] {'seq'}, use_global_device_ids=true, to_apply=%region_18.19 | all-reduce | flops 384 | bytes 3072 | tf_op jit(solution)/shard_map/psum | solution.py:153
  976.7 1.4 fusion.63
  978.1 1.4 fusion.65
  979.6 295.4 %all-reduce.10.cloned.1.call-done = (f32[384,768]{1,0:T(8,128)}, f32[384,768]{1,0:T(8,128)}) async-done(((f32[384,768]{1,0:T(8,128)}, f32[384,768]{1,0:T(8,128)}), (f32[384,768]{1,0:T(8,128)}, f32[384,768]{1,0:T(8,128)})) %all-reduce.10.cloned.1.call-update) | async-done | bytes 2359312 | tf_op jit(solution)/shard_map/psum | solution.py:157
  1275.1 2.1 fusion.8
  1277.2 30.1 %psum.109 = f32[384,32]{0,1:T(8,128)S(1)} all-reduce(f32[384,32]{0,1:T(8,128)S(1)} %fusion.8), channel_id=1, replica_groups=mesh['seq'=64,'tp'=8] {'tp'}, use_global_device_ids=true, to_apply=%region_21.22 | all-reduce | flops 12288 | bytes 98304 | tf_op jit(solution)/shard_map/psum | solution.py:166
  1307.3 112.8 %psum.110 = f32[384]{0:T(512)S(1)} all-reduce(f32[384]{0:T(512)S(1)} %get-tuple-element.19), channel_id=1, replica_groups=mesh['seq'=64,'tp'=8] {'seq'}, use_global_device_ids=true, to_apply=%region_23.24 | all-reduce | flops 384 | bytes 3072 | tf_op jit(solution)/shard_map/psum | solution.py:169
  1421.9 1.7 fusion.1
  1423.5 1.6 fusion
  1425.1 148.8 %all-gather.2.cloned.1.call-done = bf16[384,2048]{0,1:T(8,128)(2,1)} async-done(((bf16[384,32]{0,1:T(8,128)(2,1)}), bf16[384,2048]{0,1:T(8,128)(2,1)}) %all-gather.2.cloned.1.call-update) | async-done | bytes 1572880 | tf_op jit(solution)/shard_map/all_gather | solution.py:174
  1573.9 2.2 fusion.93
  1576.1 109.6 %pmax.15 = f32[384]{0:T(512)S(1)} all-reduce(f32[384]{0:T(512)S(1)} %get-tuple-element.41), channel_id=1, replica_groups=mesh['seq'=64,'tp'=8] {'seq','tp'}, use_global_device_ids=true, to_apply=%region_25.26 | all-reduce | flops 384 | bytes 3072 | tf_op jit(solution)/shard_map/pmax | solution.py:179
  1685.8 98.8 %psum.111 = f32[384]{0:T(512)S(1)} all-reduce(f32[384]{0:T(512)S(1)} %exponential_reduce_fusion), channel_id=1, replica_groups=mesh['seq'=64,'tp'=8] {'seq','tp'}, use_global_device_ids=true, to_apply=%region_27.28 | all-reduce | flops 384 | bytes 3072 | tf_op jit(solution)/shard_map/psum | solution.py:180
  (108 shorter events, 15.6 us)
Async XLA Ops:
  7.2 1566.7 %copy-start = (bf16[2048,256]{1,0:T(8,128)(2,1)S(1)}, bf16[2048,256]{1,0:T(8,128)(2,1)}, u32[]{:S(2)}) copy-start(bf16[2048,256]{1,0:T(8,128)(2,1)} %param.35) | copy-start | bytes 3145732
  7.2 400.6 %all-reduce.8.cloned.1.call-start = ((), (), s32[]{:S(2)}) async-start(), calls=%async_computation | async-start | bytes 786432 | tf_op jit(solution)/shard_map/psum | solution.py:99
  132.7 689.1 %all-reduce.12.cloned.1.call-start = ((), (), s32[]{:S(2)}) async-start(), calls=%async_computation.3 | async-start | bytes 1966080 | tf_op jit(solution)/shard_map/psum | solution.py:129
  134.6 1.4 copy-start.12
  134.6 1.6 copy-start.1
  134.6 1.6 copy-start.8
  134.6 1.6 copy-start.9
  135.0 2.7 copy-start.7
  135.3 273.5 %copy-start.16 = (f32[128]{0:T(128)S(1)}, f32[128]{0:T(128)}, u32[]{:S(2)}) copy-start(f32[128]{0:T(128)} %param.27) | copy-start | bytes 1540
  410.4 1.0 copy-start.2
  411.4 115.0 %copy-start.3 = (bf16[8,256,128]{2,1,0:T(8,128)(2,1)S(1)}, bf16[8,256,128]{2,1,0:T(8,128)(2,1)}, u32[]{:S(2)}) copy-start(bf16[8,256,128]{2,1,0:T(8,128)(2,1)} %param.38) | copy-start | bytes 1572868
  526.5 1.2 copy-start.10
  527.6 295.3 %copy-start.13 = (f32[128]{0:T(128)S(1)}, f32[128]{0:T(128)}, u32[]{:S(2)}) copy-start(f32[128]{0:T(128)} %param.28) | copy-start | bytes 1540
  527.6 747.5 %all-reduce.10.cloned.1.call-start = ((), (), s32[]{:S(2)}) async-start(), calls=%async_computation.2 | async-start | bytes 4718592 | tf_op jit(solution)/shard_map/psum | solution.py:157
  822.9 2.5 copy-start.18
  826.0 150.7 %copy-start.5 = (bf16[32,768]{1,0:T(8,128)(2,1)S(1)}, bf16[32,768]{1,0:T(8,128)(2,1)}, u32[]{:S(2)}) copy-start(bf16[32,768]{1,0:T(8,128)(2,1)} %param.32) | copy-start | bytes 147460
  826.0 150.7 %copy-start.11 = (f32[32]{0:T(128)S(1)}, f32[32]{0:T(128)}, u32[]{:S(2)}) copy-start(f32[32]{0:T(128)} %param.30) | copy-start | bytes 388
  826.7 151.5 %copy-start.6 = (bf16[32,768]{1,0:T(8,128)(2,1)S(1)}, bf16[32,768]{1,0:T(8,128)(2,1)}, u32[]{:S(2)}) copy-start(bf16[32,768]{1,0:T(8,128)(2,1)} %param.31) | copy-start | bytes 147460
  979.5 295.5 %copy-start.19 = (bf16[768,32]{0,1:T(8,128)(2,1)S(1)}, bf16[768,32]{0,1:T(8,128)(2,1)}, u32[]{:S(2)}) copy-start(bf16[768,32]{0,1:T(8,128)(2,1)} %param.33) | copy-start | bytes 147460
  979.6 594.3 %all-gather.2.cloned.1.call-start = ((), (), s32[]{:S(2)}) async-start(), calls=%async_computation.1 | async-start | bytes 1597440 | tf_op jit(solution)/shard_map/all_gather | solution.py:174
  1275.0 145.0 %copy-start.14 = (f32[32]{0:T(128)S(1)}, f32[32]{0:T(128)}, u32[]{:S(2)}) copy-start(f32[32]{0:T(128)} %param.34) | copy-start | bytes 388
  1275.0 145.7 %copy-start.15 = (f32[8]{0:T(128)S(1)}, f32[8]{0:T(128)}, u32[]{:S(2)}) copy-start(f32[8]{0:T(128)} %param.36) | copy-start | bytes 100
  1275.0 146.0 %copy-start.21 = (s32[8]{0:T(128)S(1)}, s32[8]{0:T(128)}, u32[]{:S(2)}) copy-start(s32[8]{0:T(128)} %param.41) | copy-start | bytes 100
  1307.3 117.8 %copy-start.4 = (bf16[384,32]{0,1:T(8,128)(2,1)}, bf16[384,32]{0,1:T(8,128)(2,1)S(1)}, u32[]{:S(2)}) copy-start(bf16[384,32]{0,1:T(8,128)(2,1)S(1)} %get-tuple-element.20) | copy-start | bytes 73732
  (2 other events, 2.0 us)
Sparse Core Ops, SparseCore 0:
  132.9 274.8 all-reduce.7
  527.7 294.0 all-reduce.11
  979.7 295.2 all-reduce.9
  1420.9 152.9 all-gather.1
where the time goes:
time: 1790 us
  blocking collectives  958 us (54%)
  waiting for transfers between devices  788 us (44%)
  matrix products  19.9 us (1%)
    psum x1, waiting for transfers between devices, on_device(): lax.psum((jnp.dot(normed2, w_gate, preferred_element_type=jnp.float32), j...  295 us
    psum x1, waiting for transfers between devices, on_device(): lax.psum((jnp.dot(normed1, wq, preferred_element_type=jnp.float32), jnp.d...  269 us
    psum x1, blocking collectives, on_device(): lax.psum((jnp.dot(normed1, wq, preferred_element_type=jnp.float32), jnp.d...  219 us
    all_gather x1, waiting for transfers between devices, on_device(): lax.all_gather(normed3, 'seq', axis=1, tiled=True)  149 us
    psum x1, blocking collectives, on_device(): squares = lax.psum(jnp.sum(hidden_wide * hidden_wide, axis=1), 'seq')  123 us
    pmax x1, blocking collectives, on_device(): cache_peak = lax.pmax(local_peak, 'seq')  114 us
    psum x1, blocking collectives, on_device(): squares_last = lax.psum(jnp.sum(next_wide * next_wide, axis=1), 'seq')  113 us
    psum x1, blocking collectives, on_device(): squares_mid = lax.psum(jnp.sum(middle_wide * middle_wide, axis=1), 'seq')  110 us
  transfers between devices with their start and end apart: 4, of which 4 were waited for; matrix products, arithmetic and copies ran while one was open for 1% of the time, Pallas kernels for 0%

commit v1 on v0

--- a/solution.py
+++ b/solution.py
@@ -6,6 +6,13 @@
 EPSILON = 1e-06
 ROPE_BASE = 1000000.0
 NEGATIVE = -1e30
+
+
+def swapped_in(x, mesh_axis, along):
+    count = lax.axis_size(mesh_axis)
+    blocks = jnp.stack([x for _ in range(count)])
+    blocks = lax.all_to_all(blocks, mesh_axis, split_axis=0, concat_axis=0)
+    return jnp.concatenate(blocks, axis=along)
 
 
 def ancestry(parents):
@@ -170,11 +177,7 @@
     normed3 = (
         next_wide * lax.rsqrt(squares_last / model_width + EPSILON)[:, None] * last_gain
     ).astype(jnp.bfloat16)
-    logits = jnp.dot(
-        lax.all_gather(normed3, "seq", axis=1, tiled=True),
-        head_weight,
-        preferred_element_type=jnp.float32,
-    )
+    logits = jnp.dot(swapped_in(normed3, "seq", 1), head_weight, preferred_element_type=jnp.float32)
     logits = logits * jnp.repeat(inv_temp, tree_size)[:, None]
     vocab_top = lax.pmax(jnp.max(logits, axis=1), ("seq", "tp"))
     vocab_total = lax.psum(jnp.sum(jnp.exp(logits - vocab_top[:, None]), axis=1), ("seq", "tp"))

time: 1790 us -> 1720 us (0.961)
  waiting for transfers between devices: 788 us -> 676 us
  blocking collectives: 958 us -> 985 us
    all_gather x1 -> x0, waiting for transfers between devices: 149 us -> none  [on_device(): lax.all_gather(normed3, 'seq', axis=1, tiled=True)]
    all_to_all x0 -> x1, waiting for transfers between devices: none -> 36.7 us  [swapped_in(): blocks = lax.all_to_all(blocks, mesh_axis, split_axis=0, concat_axis=0)]
    pmax x1, blocking collectives: 110 us -> 136 us  [on_device(): vocab_top = lax.pmax(jnp.max(logits, axis=1), ('seq', 'tp'))]
where the time goes in v1:
time: 1720 us
  blocking collectives  985 us (57%)
  waiting for transfers between devices  676 us (39%)
  matrix products  19.4 us (1%)
    psum x1, waiting for transfers between devices, on_device(): lax.psum((jnp.dot(normed2, w_gate, preferred_element_type=jnp.float32), j...  295 us
    psum x1, waiting for transfers between devices, on_device(): lax.psum((jnp.dot(normed1, wq, preferred_element_type=jnp.float32), jnp.d...  269 us
    psum x1, blocking collectives, on_device(): lax.psum((jnp.dot(normed1, wq, preferred_element_type=jnp.float32), jnp.d...  219 us
    pmax x1, blocking collectives, on_device(): vocab_top = lax.pmax(jnp.max(logits, axis=1), ('seq', 'tp'))  136 us
    psum x1, blocking collectives, on_device(): squares = lax.psum(jnp.sum(hidden_wide * hidden_wide, axis=1), 'seq')  123 us
    pmax x1, blocking collectives, on_device(): cache_peak = lax.pmax(local_peak, 'seq')  114 us
    psum x1, blocking collectives, on_device(): squares_last = lax.psum(jnp.sum(next_wide * next_wide, axis=1), 'seq')  113 us
    psum x1, blocking collectives, on_device(): squares_mid = lax.psum(jnp.sum(middle_wide * middle_wide, axis=1), 'seq')  110 us
  transfers between devices with their start and end apart: 4, of which 4 were waited for; matrix products, arithmetic and copies ran while one was open for 1% of the time, Pallas kernels for 0%

profile of v1, /device:TPU:1, one launch (start us, length us, event | category | flops | bytes accessed | tf_op | source)
XLA Modules:
  0.0 1717.7 jit_solution(9531586859415638643)
XLA Ops:
  8.1 122.9 %psum.98 = f32[384]{0:T(512)S(1)} all-reduce(f32[384]{0:T(512)S(1)} %fusion.51), channel_id=1, replica_groups=mesh['seq'=64,'tp'=8] {'seq'}, use_global_device_ids=true, to_apply=%region_1.0 | all-reduce | flops 384 | bytes 3072 | tf_op jit(solution)/shard_map/psum | solution.py:102
  130.9 1.8 fusion.88
  132.8 1.4 convolution_minimum_fusion.5
  138.7 269.0 %all-reduce.8.cloned.1.call-done = f32[384,2,128]{0,2,1:T(8,128)} async-done(((f32[384,2,128]{0,2,1:T(8,128)}), f32[384,2,128]{0,2,1:T(8,128)}) %all-reduce.8.cloned.1.call-update) | async-done | bytes 393232 | tf_op jit(solution)/shard_map/psum | solution.py:106
  408.8 1.1 multiply_multiply_fusion
  411.8 114.2 %pmax.14 = f32[8,1,2,48]{3,2,0,1:T(2,128)S(1)} all-reduce(f32[8,1,2,48]{3,2,0,1:T(2,128)S(1)} %bitcast.138), channel_id=1, replica_groups=mesh['seq'=64,'tp'=8] {'seq'}, use_global_device_ids=true, to_apply=%region_6.0 | all-reduce | flops 768 | bytes 6144 | tf_op jit(solution)/shard_map/pmax | solution.py:134
  528.0 219.3 %all-reduce.13 = (bf16[384,128]{1,0:T(8,128)(2,1)S(1)}, f32[8,1,2,48]{3,2,0,1:T(2,128)S(1)}) all-reduce(f32[384,128]{1,0:T(8,128)S(1)} %fusion.84, f32[8,1,2,48]{3,2,0,1:T(2,128)S(1)} %get-tuple-element.32), channel_id=1, replica_groups=mesh['seq'=64,'tp'=8] {'seq'}, use_global_device_ids=true, to_apply=%region_11.12 | all-reduce | flops 49920 | bytes 301056 | tf_op jit(solution)/shard_map/psum | solution.py:106
  747.3 74.5 %all-reduce.12.cloned.1.call-done = (f32[8,1,2,48,128]{4,3,2,0,1:T(8,128)}, f32[384,128]{1,0:T(8,128)}, f32[384,256]{1,0:T(8,128)}) async-done(((f32[8,1,2,48,128]{4,3,2,0,1:T(8,128)}, f32[384,128]{1,0:T(8,128)}, f32[384,256]{1,0:T(8,128)}), (f32[8,1,2,48,128]{4,3,2,0,1:T(8,128)}, f32[384,128]{1,0:T(8,128)}, f32[384,256]{1,0:T(8,128)})) %all-reduce.12.cloned.1.call-update) | async-done | bytes 983056 | tf_op jit(solution)/shard_map/psum | solution.py:136
  826.7 39.9 %psum.105 = f32[384,32]{0,1:T(8,128)S(1)} all-reduce(f32[384,32]{0,1:T(8,128)S(1)} %fusion.43), channel_id=1, replica_groups=mesh['seq'=64,'tp'=8] {'tp'}, use_global_device_ids=true, to_apply=%region_16.17 | all-reduce | flops 12288 | bytes 98304 | tf_op jit(solution)/shard_map/psum | solution.py:157
  866.6 110.1 %psum.106 = f32[384]{0:T(512)S(1)} all-reduce(f32[384]{0:T(512)S(1)} %get-tuple-element.21), channel_id=1, replica_groups=mesh['seq'=64,'tp'=8] {'seq'}, use_global_device_ids=true, to_apply=%region_18.19 | all-reduce | flops 384 | bytes 3072 | tf_op jit(solution)/shard_map/psum | solution.py:160
  976.7 1.4 fusion.63
  978.2 1.4 fusion.65
  979.6 295.5 %all-reduce.10.cloned.1.call-done = (f32[384,768]{1,0:T(8,128)}, f32[384,768]{1,0:T(8,128)}) async-done(((f32[384,768]{1,0:T(8,128)}, f32[384,768]{1,0:T(8,128)}), (f32[384,768]{1,0:T(8,128)}, f32[384,768]{1,0:T(8,128)})) %all-reduce.10.cloned.1.call-update) | async-done | bytes 2359312 | tf_op jit(solution)/shard_map/psum | solution.py:164
  1275.1 2.1 fusion.8
  1277.2 30.1 %psum.109 = f32[384,32]{0,1:T(8,128)S(1)} all-reduce(f32[384,32]{0,1:T(8,128)S(1)} %fusion.8), channel_id=1, replica_groups=mesh['seq'=64,'tp'=8] {'tp'}, use_global_device_ids=true, to_apply=%region_21.22 | all-reduce | flops 12288 | bytes 98304 | tf_op jit(solution)/shard_map/psum | solution.py:173
  1307.3 112.8 %psum.110 = f32[384]{0:T(512)S(1)} all-reduce(f32[384]{0:T(512)S(1)} %get-tuple-element.19), channel_id=1, replica_groups=mesh['seq'=64,'tp'=8] {'seq'}, use_global_device_ids=true, to_apply=%region_23.24 | all-reduce | flops 384 | bytes 3072 | tf_op jit(solution)/shard_map/psum | solution.py:176
  1420.2 1.3 stack.2
  1421.5 8.0 all-to-all-start
  1431.1 1.5 gather_fusion
  1432.8 2.6 fusion.1
  1435.4 1.6 fusion
  1436.9 36.7 %all-to-all-done = bf16[64,384,32]{1,2,0:T(8,128)(2,1)S(1)} async-done(((bf16[64,384,32]{1,2,0:T(8,128)(2,1)}), bf16[64,384,32]{1,2,0:T(8,128)(2,1)S(1)}, u32[]{:S(2)}, u32[]{:S(2)}) %all-to-all-start) | async-done | bytes 1572896 | tf_op jit(solution)/shard_map/all_to_all | solution.py:14
  1474.4 136.3 %pmax.15 = f32[384]{0:T(512)S(1)} all-reduce(f32[384]{0:T(512)S(1)} %get-tuple-element.41), channel_id=1, replica_groups=mesh['seq'=64,'tp'=8] {'seq','tp'}, use_global_device_ids=true, to_apply=%region_25.26 | all-reduce | flops 384 | bytes 3072 | tf_op jit(solution)/shard_map/pmax | solution.py:182
  1610.8 99.4 %psum.111 = f32[384]{0:T(512)S(1)} all-reduce(f32[384]{0:T(512)S(1)} %exponential_reduce_fusion), channel_id=1, replica_groups=mesh['seq'=64,'tp'=8] {'seq','tp'}, use_global_device_ids=true, to_apply=%region_27.28 | all-reduce | flops 384 | bytes 3072 | tf_op jit(solution)/shard_map/psum | solution.py:183
  (108 shorter events, 18.6 us)
Async XLA Ops:
  7.2 1466.5 %copy-start = (bf16[2048,256]{1,0:T(8,128)(2,1)S(1)}, bf16[2048,256]{1,0:T(8,128)(2,1)}, u32[]{:S(2)}) copy-start(bf16[2048,256]{1,0:T(8,128)(2,1)} %param.35) | copy-start | bytes 3145732
  7.2 400.6 %all-reduce.8.cloned.1.call-start = ((), (), s32[]{:S(2)}) async-start(), calls=%async_computation.1 | async-start | bytes 786432 | tf_op jit(solution)/shard_map/psum | solution.py:106
  132.7 689.1 %all-reduce.12.cloned.1.call-start = ((), (), s32[]{:S(2)}) async-start(), calls=%async_computation.3 | async-start | bytes 1966080 | tf_op jit(solution)/shard_map/psum | solution.py:136
  134.6 1.4 copy-start.12
  134.6 1.6 copy-start.1
  134.6 1.6 copy-start.8
  134.6 1.6 copy-start.9
  135.0 2.7 copy-start.7
  135.3 273.5 %copy-start.16 = (f32[128]{0:T(128)S(1)}, f32[128]{0:T(128)}, u32[]{:S(2)}) copy-start(f32[128]{0:T(128)} %param.27) | copy-start | bytes 1540
  410.4 1.0 copy-start.2
  411.4 115.0 %copy-start.3 = (bf16[8,256,128]{2,1,0:T(8,128)(2,1)S(1)}, bf16[8,256,128]{2,1,0:T(8,128)(2,1)}, u32[]{:S(2)}) copy-start(bf16[8,256,128]{2,1,0:T(8,128)(2,1)} %param.38) | copy-start | bytes 1572868
  526.5 1.2 copy-start.10
  527.5 295.3 %copy-start.13 = (f32[128]{0:T(128)S(1)}, f32[128]{0:T(128)}, u32[]{:S(2)}) copy-start(f32[128]{0:T(128)} %param.28) | copy-start | bytes 1540
  527.6 747.5 %all-reduce.10.cloned.1.call-start = ((), (), s32[]{:S(2)}) async-start(), calls=%async_computation.2 | async-start | bytes 4718592 | tf_op jit(solution)/shard_map/psum | solution.py:164
  747.3 79.3 %copy-start.19 = (bf16[384,128]{1,0:T(8,128)(2,1)}, bf16[384,128]{1,0:T(8,128)(2,1)S(1)}, u32[]{:S(2)}) copy-start(bf16[384,128]{1,0:T(8,128)(2,1)S(1)} %get-tuple-element.12) | copy-start | bytes 294916
  822.9 2.5 copy-start.18
  826.0 150.7 %copy-start.5 = (bf16[32,768]{1,0:T(8,128)(2,1)S(1)}, bf16[32,768]{1,0:T(8,128)(2,1)}, u32[]{:S(2)}) copy-start(bf16[32,768]{1,0:T(8,128)(2,1)} %param.32) | copy-start | bytes 147460
  826.0 150.7 %copy-start.11 = (f32[32]{0:T(128)S(1)}, f32[32]{0:T(128)}, u32[]{:S(2)}) copy-start(f32[32]{0:T(128)} %param.30) | copy-start | bytes 388
  826.7 151.5 %copy-start.6 = (bf16[32,768]{1,0:T(8,128)(2,1)S(1)}, bf16[32,768]{1,0:T(8,128)(2,1)}, u32[]{:S(2)}) copy-start(bf16[32,768]{1,0:T(8,128)(2,1)} %param.31) | copy-start | bytes 147460
  979.6 295.5 %copy-start.20 = (bf16[768,32]{0,1:T(8,128)(2,1)S(1)}, bf16[768,32]{0,1:T(8,128)(2,1)}, u32[]{:S(2)}) copy-start(bf16[768,32]{0,1:T(8,128)(2,1)} %param.33) | copy-start | bytes 147460
  1275.1 145.0 %copy-start.14 = (f32[32]{0:T(128)S(1)}, f32[32]{0:T(128)}, u32[]{:S(2)}) copy-start(f32[32]{0:T(128)} %param.34) | copy-start | bytes 388
  1307.3 114.2 %copy-start.4 = (bf16[384,32]{0,1:T(8,128)(2,1)}, bf16[384,32]{0,1:T(8,128)(2,1)S(1)}, u32[]{:S(2)}) copy-start(bf16[384,32]{0,1:T(8,128)(2,1)S(1)} %get-tuple-element.20) | copy-start | bytes 73732
  1421.5 8.0 copy-start.15
  1421.5 52.2 %all-to-all-start = ((bf16[64,384,32]{1,2,0:T(8,128)(2,1)}), bf16[64,384,32]{1,2,0:T(8,128)(2,1)S(1)}, u32[]{:S(2)}, u32[]{:S(2)}) async-start(bf16[64,384,32]{1,2,0:T(8,128)(2,1)} %stack.2), calls=%async_computation | async-start | bytes 3145728 | tf_op jit(solution)/shard_map/all_to_all | solution.py:14
  (2 other events, 2.0 us)
Sparse Core Ops, SparseCore 0:
  132.9 274.8 all-reduce.7
  527.7 294.0 all-reduce.11
  979.7 295.3 all-reduce.9
